TPU v7x, 32 devices: a whole 2x2x4 slice. The times are simulated.
32 devices in a mesh: seq: 8 (over y, x, core), tp: 4 (over z).
Axes of the slice: x: 2, y: 2, z: 4, core: 2. Of those that a mesh axis runs over, the one named last changes fastest.
Arguments:
- tokens: bfloat16 [128, 17, 1152], P('seq'), may hold values from -6 to 6
- cotangent: bfloat16 [128, 17, 1152], P('seq'), may hold values from -6 to 6
- caption: bfloat16 [4, 300, 1152], replicated, may hold values from -6 to 6
- condition: float32 [4, 1152], replicated, may hold values from -6 to 6
- frames: int32 [4], replicated, may hold values from 1 to 17, 44 in all
- cap_len: int32 [4], replicated, may hold values from 1 to 300, 600 in all
- clip_of: int32 [128], P('seq'), may hold values from 0 to 3
- w_qkv: bfloat16 [1152, 3, 1152], P('seq', None, 'tp'), may hold values from -0.1875 to 0.1875
- w_out: bfloat16 [1152, 1152], P('tp', 'seq'), may hold values from -0.375 to 0.375
- w_query2: bfloat16 [1152, 1152], P('seq', 'tp'), may hold values from -0.1875 to 0.1875
- w_kv2: bfloat16 [1152, 2, 1152], P('seq', None, 'tp'), may hold values from -0.1875 to 0.1875
- w_out2: bfloat16 [1152, 1152], P('tp', 'seq'), may hold values from -0.75 to 0.75
- w_up: bfloat16 [1152, 4608], P('seq', 'tp'), may hold values from -0.1875 to 0.1875
- w_down: bfloat16 [4608, 1152], P('tp', 'seq'), may hold values from -0.09375 to 0.09375
- w_ada: bfloat16 [1152, 6912], P('seq', 'tp'), may hold values from -0.1875 to 0.1875
Outputs:
- output: bfloat16 [128, 17, 1152], P('seq')
- d_tokens: bfloat16 [128, 17, 1152], P('seq')
- d_caption: float32 [4, 300, 1152], P(None, None, 'tp')
- d_condition: float32 [4, 1152], replicated
- d_w_qkv: float32 [1152, 3, 1152], P('seq', None, 'tp')
- d_w_out: float32 [1152, 1152], P('tp', 'seq')
- d_w_query2: float32 [1152, 1152], P('seq', 'tp')
- d_w_kv2: float32 [1152, 2, 1152], P('seq', None, 'tp')
- d_w_out2: float32 [1152, 1152], P('tp', 'seq')
- d_w_up: float32 [1152, 4608], P('seq', 'tp')
- d_w_down: float32 [4608, 1152], P('tp', 'seq')
- d_w_ada: float32 [1152, 6912], P('seq', 'tp')
Inputs may be any that keep to these rules, and one draw needn't show every extreme that they name: frames of each clip; they add up to 44 and one clip has 17. `cap_len`: live caption tokens of each clip, the first ones of its slots; they add up to 600 and one clip has 300.
All inputs are finite; a program needn't handle non-finite values.
Results may differ from a plain program's by a relative error of at most 0.024.
Values may be sent and summed in bfloat16 or wider, within the bound.
No kernel may reach another device: no remote copies, remote signals or barrier semaphores. Data moves between devices by JAX's collectives and lax.ppermute only.
A program may use at most 128 MiB of HBM per device.

v0:
```python
import jax
import jax.numpy as jnp
from jax import lax
from jax.sharding import PartitionSpec as P

HDIM = 72
CLIPS = 4
EPSILON = 1e-06
NEG_FILL = -1e30
HIGHEST = lax.Precision.HIGHEST


def normalize(rows):
    center = rows - jnp.mean(rows, -1, keepdims=True)
    return center * lax.rsqrt(jnp.mean(center * center, -1, keepdims=True) + EPSILON)


def modulate(rows, shift, scale):
    return normalize(rows) * (1.0 + scale[:, None, :]) + shift[:, None, :]


def total_rows(partial_value):
    return lax.psum(partial_value, "tp")


def frame_attention(triple, live, head_scale):
    raw = (
        jnp.einsum(
            "lfhe,lghe->lhfg", triple[:, :, 0], triple[:, :, 1], preferred_element_type=jnp.float32
        )
        * head_scale
    )
    probs = jax.nn.softmax(jnp.where(live[:, None, None, :], raw, NEG_FILL), axis=-1)
    result = jnp.einsum(
        "lhfg,lghe->lfhe",
        probs.astype(jnp.bfloat16),
        triple[:, :, 2],
        preferred_element_type=jnp.float32,
    )
    return (probs, result.astype(jnp.bfloat16))


def cross_scores(query, keys, clips, key_clip, key_live, head_scale):
    raw = jnp.einsum("rhe,khe->hrk", query, keys, preferred_element_type=jnp.float32) * head_scale
    allowed = (clips[:, None] == key_clip[None, :]) & key_live[None, :]
    return jnp.where(allowed[None], raw, NEG_FILL)


def shards(
    tokens,
    cotangent,
    caption,
    condition,
    frames,
    cap_len,
    clip_of,
    w_qkv,
    w_out,
    w_query2,
    w_kv2,
    w_out2,
    w_up,
    w_down,
    w_ada,
):
    seqs, fmax, width = tokens.shape
    row_count = seqs * fmax
    inner = w_qkv.shape[2]
    local_heads = inner // HDIM
    head_scale = HDIM ** (-0.5)
    full_qkv, full_out, full_query2, full_kv2, full_out2, full_up, full_down, full_ada = (
        lax.all_gather(w_qkv, "seq", axis=0, tiled=True),
        lax.all_gather(w_out, "seq", axis=1, tiled=True),
        lax.all_gather(w_query2, "seq", axis=0, tiled=True),
        lax.all_gather(w_kv2, "seq", axis=0, tiled=True),
        lax.all_gather(w_out2, "seq", axis=1, tiled=True),
        lax.all_gather(w_up, "seq", axis=0, tiled=True),
        lax.all_gather(w_down, "seq", axis=1, tiled=True),
        lax.all_gather(w_ada, "seq", axis=0, tiled=True),
    )
    qkv_matrix = full_qkv.reshape(width, 3 * inner)
    kv_matrix = full_kv2.reshape(width, 2 * inner)
    scaled = jax.nn.silu(condition).astype(jnp.bfloat16)
    mod_part = jnp.dot(scaled, full_ada, preferred_element_type=jnp.float32)
    mods = lax.all_gather(mod_part, "tp", axis=1, tiled=True).reshape(CLIPS, 6, width)
    clip_ids = jnp.arange(CLIPS)
    clip_hot = clip_of[:, None] == clip_ids[None, :]
    seq_mods = jnp.sum(jnp.where(clip_hot[:, :, None, None], mods[None], 0.0), 1)
    seq_frames = jnp.sum(jnp.where(clip_hot, frames[None, :], 0), 1)
    live = jnp.arange(fmax)[None, :] < seq_frames[:, None]
    own_live = live.astype(jnp.float32)[:, :, None]
    own_hot = clip_hot.astype(jnp.float32)
    key_count = caption.shape[0] * caption.shape[1]
    key_clip = jnp.arange(key_count) // caption.shape[1]
    key_len = jnp.sum(jnp.where(key_clip[:, None] == clip_ids[None, :], cap_len[None, :], 0), 1)
    key_live = jnp.arange(key_count) % caption.shape[1] < key_len
    row_clip = jnp.repeat(clip_of, fmax)
    block_seqs = min(32, seqs)
    blocks = seqs // block_seqs
    block_rows = block_seqs * fmax
    block_clip = row_clip.reshape(blocks, block_rows)
    own_input = tokens.astype(jnp.float32)
    attn_in = (
        modulate(own_input, seq_mods[:, 0], seq_mods[:, 1])
        .astype(jnp.bfloat16)
        .reshape(row_count, width)
    )
    triple = (
        jnp.dot(attn_in, qkv_matrix, preferred_element_type=jnp.float32)
        .astype(jnp.bfloat16)
        .reshape(seqs, fmax, 3, local_heads, HDIM)
    )
    probs, frame_out = frame_attention(triple, live, head_scale)
    frame_out = frame_out.reshape(row_count, inner)
    branch_one = total_rows(
        jnp.dot(frame_out, full_out, preferred_element_type=jnp.float32).reshape(seqs, fmax, width)
    )
    first = own_input + seq_mods[:, 2][:, None, :] * branch_one
    first_low = first.astype(jnp.bfloat16).reshape(row_count, width)
    cross_query = (
        jnp.dot(first_low, full_query2, preferred_element_type=jnp.float32)
        .astype(jnp.bfloat16)
        .reshape(blocks, block_rows, local_heads, HDIM)
    )
    cross_kv = (
        jnp.dot(caption.reshape(key_count, width), kv_matrix, preferred_element_type=jnp.float32)
        .astype(jnp.bfloat16)
        .reshape(key_count, 2, local_heads, HDIM)
    )
    cross_key = cross_kv[:, 0]
    cross_value = cross_kv[:, 1]

    def cross_block(pair):
        query, clips = pair
        scores = cross_scores(query, cross_key, clips, key_clip, key_live, head_scale)
        top = jnp.max(scores, -1, keepdims=True)
        weights = jnp.exp(scores - top)
        denom = jnp.sum(weights, -1, keepdims=True)
        block_out = jnp.einsum(
            "hrk,khe->rhe",
            (weights / denom).astype(jnp.bfloat16),
            cross_value,
            preferred_element_type=jnp.float32,
        )
        return (block_out.astype(jnp.bfloat16), (top + jnp.log(denom))[..., 0])

    cross_out, cross_lse = lax.map(cross_block, (cross_query, block_clip))
    cross_out = cross_out.reshape(row_count, inner)
    second = first + total_rows(
        jnp.dot(cross_out, full_out2, preferred_element_type=jnp.float32).reshape(seqs, fmax, width)
    )
    mlp_in = (
        modulate(second, seq_mods[:, 3], seq_mods[:, 4])
        .astype(jnp.bfloat16)
        .reshape(row_count, width)
    )
    hidden_pre = jnp.dot(mlp_in, full_up, preferred_element_type=jnp.float32)
    hidden = jax.nn.gelu(hidden_pre, approximate=True).astype(jnp.bfloat16)
    branch_three = total_rows(
        jnp.dot(hidden, full_down, preferred_element_type=jnp.float32).reshape(seqs, fmax, width)
    )
    third = second + seq_mods[:, 5][:, None, :] * branch_three
    output = (third * own_live).astype(jnp.bfloat16)
    grad_three = cotangent.astype(jnp.float32) * own_live
    d_branch3 = (
        (seq_mods[:, 5][:, None, :] * grad_three).astype(jnp.bfloat16).reshape(row_count, width)
    )
    grad_down = jnp.einsum("rk,rd->kd", hidden, d_branch3, preferred_element_type=jnp.float32)
    d_hidden = jnp.einsum("rd,kd->rk", d_branch3, full_down, preferred_element_type=jnp.float32)
    gelu_pull = jax.vjp(lambda value: jax.nn.gelu(value, approximate=True), hidden_pre)[1]
    d_pre = gelu_pull(d_hidden)[0].astype(jnp.bfloat16)
    grad_up = jnp.einsum("rd,rk->dk", mlp_in, d_pre, preferred_element_type=jnp.float32)
    d_mlp = total_rows(
        jnp.einsum("rk,dk->rd", d_pre, full_up, preferred_element_type=jnp.float32).reshape(
            seqs, fmax, width
        )
    )
    second_pull = jax.vjp(modulate, second, seq_mods[:, 3], seq_mods[:, 4])[1]
    norm_two, d_shift2, d_scale2 = second_pull(d_mlp)
    grad_two = grad_three + norm_two
    d_branch2 = grad_two.astype(jnp.bfloat16).reshape(row_count, width)
    grad_out2 = jnp.einsum("rc,rd->cd", cross_out, d_branch2, preferred_element_type=jnp.float32)
    d_cross = (
        jnp.einsum("rd,cd->rc", d_branch2, full_out2, preferred_element_type=jnp.float32)
        .astype(jnp.bfloat16)
        .reshape(blocks, block_rows, local_heads, HDIM)
    )

    def cross_back(carry, item):
        key_sum, value_sum = carry
        query, clips, block_lse, grad_block = item
        scores = cross_scores(query, cross_key, clips, key_clip, key_live, head_scale)
        weights = jnp.exp(scores - block_lse[..., None])
        value_sum = value_sum + jnp.einsum(
            "hrk,rhe->khe",
            weights.astype(jnp.bfloat16),
            grad_block,
            preferred_element_type=jnp.float32,
        )
        grad_weights = jnp.einsum(
            "rhe,khe->hrk", grad_block, cross_value, preferred_element_type=jnp.float32
        )
        grad_scores = (
            weights * (grad_weights - jnp.sum(weights * grad_weights, -1, keepdims=True))
        ).astype(jnp.bfloat16)
        grad_query = (
            jnp.einsum("hrk,khe->rhe", grad_scores, cross_key, preferred_element_type=jnp.float32)
            * head_scale
        ).astype(jnp.bfloat16)
        key_sum = (
            key_sum
            + jnp.einsum("hrk,rhe->khe", grad_scores, query, preferred_element_type=jnp.float32)
            * head_scale
        )
        return ((key_sum, value_sum), grad_query)

    zero_keys = jnp.zeros((key_count, local_heads, HDIM), jnp.float32)
    (key_grad, value_grad), d_query = lax.scan(
        cross_back, (zero_keys, zero_keys), (cross_query, block_clip, cross_lse, d_cross)
    )
    d_query = d_query.reshape(row_count, inner)
    grad_query2 = jnp.einsum("rd,rc->dc", first_low, d_query, preferred_element_type=jnp.float32)
    grad_one = grad_two + total_rows(
        jnp.einsum("rc,dc->rd", d_query, full_query2, preferred_element_type=jnp.float32).reshape(
            seqs, fmax, width
        )
    )
    d_branch1 = (
        (seq_mods[:, 2][:, None, :] * grad_one).astype(jnp.bfloat16).reshape(row_count, width)
    )
    grad_out = jnp.einsum("rc,rd->cd", frame_out, d_branch1, preferred_element_type=jnp.float32)
    d_frame = (
        jnp.einsum("rd,cd->rc", d_branch1, full_out, preferred_element_type=jnp.float32)
        .astype(jnp.bfloat16)
        .reshape(seqs, fmax, local_heads, HDIM)
    )
    d_value = jnp.einsum(
        "lhfg,lfhe->lghe", probs.astype(jnp.bfloat16), d_frame, preferred_element_type=jnp.float32
    )
    d_probs = jnp.einsum(
        "lfhe,lghe->lhfg", d_frame, triple[:, :, 2], preferred_element_type=jnp.float32
    )
    d_scores = (probs * (d_probs - jnp.sum(probs * d_probs, -1, keepdims=True))).astype(
        jnp.bfloat16
    )
    d_queries = (
        jnp.einsum("lhfg,lghe->lfhe", d_scores, triple[:, :, 1], preferred_element_type=jnp.float32)
        * head_scale
    )
    d_keys = (
        jnp.einsum("lhfg,lfhe->lghe", d_scores, triple[:, :, 0], preferred_element_type=jnp.float32)
        * head_scale
    )
    d_triple = (
        jnp.stack([d_queries, d_keys, d_value], 2)
        .astype(jnp.bfloat16)
        .reshape(row_count, 3 * inner)
    )
    grad_qkv = jnp.einsum(
        "rd,rc->dc", attn_in, d_triple, preferred_element_type=jnp.float32
    ).reshape(width, 3, inner)
    d_attn = total_rows(
        jnp.einsum("rc,dc->rd", d_triple, qkv_matrix, preferred_element_type=jnp.float32).reshape(
            seqs, fmax, width
        )
    )
    first_pull = jax.vjp(modulate, own_input, seq_mods[:, 0], seq_mods[:, 1])[1]
    norm_one, d_shift1, d_scale1 = first_pull(d_attn)
    d_tokens = (grad_one + norm_one).astype(jnp.bfloat16)
    d_gate1 = jnp.sum(grad_one * branch_one, 1)
    d_gate2 = jnp.sum(grad_three * branch_three, 1)
    seq_terms = jnp.stack([d_shift1, d_scale1, d_gate1, d_shift2, d_scale2, d_gate2], 1)
    d_mods = jnp.einsum("lc,ljd->cjd", own_hot, seq_terms, precision=HIGHEST).reshape(
        CLIPS, 6 * width
    )
    kv_grad = jnp.stack([key_grad, value_grad], 1)
    kv_total, mods_total = (
        lax.psum(kv_grad.astype(jnp.bfloat16), "seq").astype(jnp.float32),
        lax.psum(d_mods.astype(jnp.bfloat16), "seq").astype(jnp.float32),
    )
    col_count = mods_total.shape[1] // lax.axis_size("tp")
    mod_cols = lax.dynamic_slice_in_dim(mods_total, lax.axis_index("tp") * col_count, col_count, 1)
    seq_rows = w_ada.shape[0]
    seq_start = lax.axis_index("seq") * seq_rows
    scaled_rows = lax.dynamic_slice_in_dim(scaled, seq_start, seq_rows, 1).astype(jnp.float32)
    grad_ada = jnp.einsum("cd,ck->dk", scaled_rows, mod_cols, precision=HIGHEST)
    silu_pull = jax.vjp(jax.nn.silu, condition)[1]
    cond_part = silu_pull(
        jnp.einsum("ck,dk->cd", mod_cols, full_ada.astype(jnp.float32), precision=HIGHEST)
    )[0]
    d_condition = lax.psum(cond_part, "tp")
    kv_low = kv_total.astype(jnp.bfloat16).reshape(key_count, 2 * inner)
    caption_rows = lax.dynamic_slice_in_dim(
        caption.reshape(key_count, width), seq_start, seq_rows, 1
    )
    grad_kv2 = jnp.einsum(
        "kd,kc->dc", caption_rows, kv_low, preferred_element_type=jnp.float32
    ).reshape(seq_rows, 2, inner)
    caption_part = jnp.einsum(
        "kc,dc->kd", kv_low, kv_matrix, preferred_element_type=jnp.float32
    ).reshape(caption.shape)
    d_caption = lax.psum_scatter(
        caption_part.astype(jnp.bfloat16), "tp", scatter_dimension=2, tiled=True
    ).astype(jnp.float32)
    summed = (
        lax.psum_scatter(
            grad_qkv.astype(jnp.bfloat16), "seq", scatter_dimension=0, tiled=True
        ).astype(jnp.float32),
        lax.psum_scatter(
            grad_out.astype(jnp.bfloat16), "seq", scatter_dimension=1, tiled=True
        ).astype(jnp.float32),
        lax.psum_scatter(
            grad_query2.astype(jnp.bfloat16), "seq", scatter_dimension=0, tiled=True
        ).astype(jnp.float32),
        lax.psum_scatter(
            grad_out2.astype(jnp.bfloat16), "seq", scatter_dimension=1, tiled=True
        ).astype(jnp.float32),
        lax.psum_scatter(
            grad_up.astype(jnp.bfloat16), "seq", scatter_dimension=0, tiled=True
        ).astype(jnp.float32),
        lax.psum_scatter(
            grad_down.astype(jnp.bfloat16), "seq", scatter_dimension=1, tiled=True
        ).astype(jnp.float32),
    )
    return (
        output,
        d_tokens,
        d_caption,
        d_condition,
        summed[0],
        summed[1],
        summed[2],
        grad_kv2,
        summed[3],
        summed[4],
        summed[5],
        grad_ada,
    )


def solution(mesh):
    return jax.shard_map(
        shards,
        mesh=mesh,
        in_specs=(
            P("seq", None, None),
            P("seq", None, None),
            P(),
            P(),
            P(),
            P(),
            P("seq"),
            P("seq", None, "tp"),
            P("tp", "seq"),
            P("seq", "tp"),
            P("seq", None, "tp"),
            P("tp", "seq"),
            P("seq", "tp"),
            P("tp", "seq"),
            P("seq", "tp"),
        ),
        out_specs=(
            P("seq", None, None),
            P("seq", None, None),
            P(None, None, "tp"),
            P(),
            P("seq", None, "tp"),
            P("tp", "seq"),
            P("seq", "tp"),
            P("seq", None, "tp"),
            P("tp", "seq"),
            P("seq", "tp"),
            P("tp", "seq"),
            P("seq", "tp"),
        ),
        check_vma=False,
    )
```

profile of v0, /device:TPU:0, one launch (start us, length us, event | category | flops | bytes accessed | tf_op | source)
XLA Modules:
  0.0 1068.3 jit_solution(13612882484881826433)
XLA Ops:
  14.8 15.0 %all_gather.30 = bf16[288,1152]{0,1:T(8,128)(2,1)S(1)} all-gather(bf16[288,144]{0,1:T(8,128)(2,1)S(1)} %copy-done.45), channel_id=1, replica_groups=mesh['seq'=8,'tp'=4] {'seq'}, dimensions={1}, use_global_device_ids=true | all-gather | bytes 746496 | tf_op jit(solution)/shard_map/all_gather | solution.py:73
  29.7 13.7 %all_gather.32 = bf16[1152,288]{1,0:T(8,128)(2,1)S(1)} all-gather(bf16[144,288]{1,0:T(8,128)(2,1)S(1)} %copy-done.46), channel_id=1, replica_groups=mesh['seq'=8,'tp'=4] {'seq'}, dimensions={0}, use_global_device_ids=true | all-gather | bytes 746496 | tf_op jit(solution)/shard_map/all_gather | solution.py:74
  43.4 11.3 %all_gather.33 = bf16[288,1152]{0,1:T(8,128)(2,1)} all-gather(bf16[288,144]{0,1:T(8,128)(2,1)S(1)} %copy-done.47), channel_id=1, replica_groups=mesh['seq'=8,'tp'=4] {'seq'}, dimensions={1}, use_global_device_ids=true | all-gather | bytes 746496 | tf_op jit(solution)/shard_map/all_gather | solution.py:76
  56.6 3.3 reshape.348
  59.9 4.3 copy.144
  64.2 21.8 %all-gather.7.cloned.1.call-done = bf16[1152,1728]{1,0:T(8,128)(2,1)} async-done(((bf16[144,1728]{1,0:T(8,128)(2,1)}), bf16[1152,1728]{1,0:T(8,128)(2,1)}) %all-gather.7.cloned.1.call-update) | async-done | bytes 3981328 | tf_op jit(solution)/shard_map/all_gather | solution.py:79
  86.0 2.8 convolution_bitcast_fusion
  88.8 13.4 %all-gather = f32[4,1728,4]{1,2,0:T(4,128)S(1)} all-gather(f32[1,1728,4]{1,2,0:T(4,128)S(1)} %convolution_bitcast_fusion), channel_id=1, replica_groups=mesh['seq'=8,'tp'=4] {'tp'}, dimensions={0}, use_global_device_ids=true | all-gather | bytes 138240 | tf_op jit(solution)/shard_map/all_gather | solution.py:85
  105.5 3.5 convolution_convert_fusion.9
  109.0 2.9 reshape.347
  115.8 2.7 fusion.37
  123.3 5.6 copy.152
  128.9 5.6 convolution_convert_fusion.4
  134.5 63.4 %all-reduce.8.cloned.1.call-done = f32[16,17,1152]{2,1,0:T(8,128)} async-done(((f32[16,17,1152]{2,1,0:T(8,128)}), f32[16,17,1152]{2,1,0:T(8,128)}) %all-reduce.8.cloned.1.call-update) | async-done | bytes 1253392 | tf_op jit(solution)/shard_map/psum | solution.py:23
  201.1 2.5 fusion.98
  212.2 73.3 %all-reduce.10.cloned.1.call-done = f32[16,17,1152]{2,1,0:T(8,128)} async-done(((f32[16,17,1152]{2,1,0:T(8,128)}), f32[16,17,1152]{2,1,0:T(8,128)}) %all-reduce.10.cloned.1.call-update) | async-done | bytes 1253392 | tf_op jit(solution)/shard_map/psum | solution.py:23
  285.5 2.5 fusion.94
  291.0 2.2 reshape.354
  293.2 2.3 reshape.352
  295.4 21.2 %all-gather.15.cloned.1.call-done = bf16[1152,1152]{0,1:T(8,128)(2,1)} async-done(((bf16[1152,144]{0,1:T(8,128)(2,1)}), bf16[1152,1152]{0,1:T(8,128)(2,1)}) %all-gather.15.cloned.1.call-update) | async-done | bytes 2654224 | tf_op jit(solution)/shard_map/all_gather | solution.py:78
  316.6 4.1 fusion.99
  320.7 28.1 %all-gather.13.cloned.1.call-done = bf16[1152,1152]{1,0:T(8,128)(2,1)} async-done(((bf16[144,1152]{1,0:T(8,128)(2,1)}), bf16[1152,1152]{1,0:T(8,128)(2,1)}) %all-gather.13.cloned.1.call-update) | async-done | bytes 2654224 | tf_op jit(solution)/shard_map/all_gather | solution.py:77
  348.8 5.0 fusion.36
  354.6 2.2 fusion.100
  356.8 2.7 reshape.355
  359.8 75.4 %all-reduce.12.cloned.1.call-done = f32[16,17,1152]{2,1,0:T(8,128)} async-done(((f32[16,17,1152]{2,1,0:T(8,128)}), f32[16,17,1152]{2,1,0:T(8,128)}) %all-reduce.12.cloned.1.call-update) | async-done | bytes 1253392 | tf_op jit(solution)/shard_map/psum | solution.py:23
  435.2 3.3 multiply_reduce_fusion.2
  441.6 2.2 reshape.356
  443.8 2.6 convolution_convert_fusion.12
  447.5 4.6 multiply_reduce_fusion
  458.0 3.1 fusion.44
  461.2 2.7 fusion.15
  463.9 4.0 fusion.16
  469.2 2.9 convolution_convert_fusion.5
  473.1 2.8 convolution_convert_fusion.6
  476.0 59.8 %all-reduce.14.cloned.1.call-done = f32[16,17,1152]{2,1,0:T(8,128)} async-done(((f32[16,17,1152]{2,1,0:T(8,128)}), f32[16,17,1152]{2,1,0:T(8,128)}) %all-reduce.14.cloned.1.call-update) | async-done | bytes 1253392 | tf_op jit(solution)/shard_map/psum | solution.py:23
  535.8 3.9 multiply_reduce_fusion.3
  542.0 2.2 reshape.357
  544.2 2.7 convolution_convert_fusion.7
  547.4 4.5 convolution_convert_fusion.1
  552.0 4.7 convolution_convert_fusion
  556.8 4.5 fusion.91
  561.3 2.7 reshape.353
  574.7 2.9 reshape.378
  577.6 4.3 fusion.101
  582.1 2.2 reshape.375
  587.4 4.5 convolution_convert_fusion.3
  591.9 4.7 all-reduce.16.cloned.1.call-done
  596.6 2.6 fusion.52
  600.2 4.2 dot_general.164
  604.5 6.6 convolution_convert_fusion.2
  611.1 23.5 %reduce-scatter.16.cloned.1.call-done = bf16[288,144]{0,1:T(8,128)(2,1)} async-done(((bf16[288,1152]{0,1:T(8,128)(2,1)}), bf16[288,144]{0,1:T(8,128)(2,1)}) %reduce-scatter.16.cloned.1.call-update) | async-done | bytes 82960 | tf_op jit(solution)/shard_map/reduce_scatter | solution.py:315
  636.2 36.7 %reduce-scatter.14.cloned.1.call-done = bf16[144,288]{1,0:T(8,128)(2,1)} async-done(((bf16[1152,288]{1,0:T(8,128)(2,1)}), bf16[144,288]{1,0:T(8,128)(2,1)}) %reduce-scatter.14.cloned.1.call-update) | async-done | bytes 82960 | tf_op jit(solution)/shard_map/reduce_scatter | solution.py:312
  674.4 37.7 %reduce-scatter.12.cloned.1.call-done = bf16[288,144]{0,1:T(8,128)(2,1)} async-done(((bf16[288,1152]{0,1:T(8,128)(2,1)}), bf16[288,144]{0,1:T(8,128)(2,1)}) %reduce-scatter.12.cloned.1.call-update) | async-done | bytes 82960 | tf_op jit(solution)/shard_map/reduce_scatter | solution.py:309
  713.7 45.6 %reduce-scatter.18.cloned.1.call-done = bf16[144,1152]{1,0:T(8,128)(2,1)} async-done(((bf16[1152,1152]{1,0:T(8,128)(2,1)}), bf16[144,1152]{1,0:T(8,128)(2,1)}) %reduce-scatter.18.cloned.1.call-update) | async-done | bytes 331792 | tf_op jit(solution)/shard_map/reduce_scatter | solution.py:318
  761.2 45.7 %reduce-scatter.20.cloned.1.call-done = bf16[1152,144]{0,1:T(8,128)(2,1)} async-done(((bf16[1152,1152]{0,1:T(8,128)(2,1)}), bf16[1152,144]{0,1:T(8,128)(2,1)}) %reduce-scatter.20.cloned.1.call-update) | async-done | bytes 331792 | tf_op jit(solution)/shard_map/reduce_scatter | solution.py:321
  808.7 135.2 %all-reduce.18.cloned.1.call-done = (f32[16,17,1152]{2,1,0:T(8,128)}, f32[16,17,1152]{2,1,0:T(8,128)}) async-done(((f32[16,17,1152]{2,1,0:T(8,128)}, f32[16,17,1152]{2,1,0:T(8,128)}), (f32[16,17,1152]{2,1,0:T(8,128)}, f32[16,17,1152]{2,1,0:T(8,128)})) %all-reduce.18.cloned.1.call-update) | async-done | bytes 2506768 | tf_op jit(solution)/shard_map/psum | solution.py:23
  943.9 2.1 fusion.25
  951.2 24.9 %psum.70 = bf16[4,6912]{1,0:T(4,128)(2,1)S(1)} all-reduce(bf16[4,6912]{1,0:T(4,128)(2,1)S(1)} %bitcast.198), channel_id=1, replica_groups=mesh['seq'=8,'tp'=4] {'seq'}, use_global_device_ids=true, to_apply=%region_31.32 | all-reduce | flops 27648 | bytes 110592 | tf_op jit(solution)/shard_map/psum | solution.py:279
  976.1 3.4 fusion.68
  979.5 17.6 %psum.71 = f32[4,1152]{1,0:T(4,128)} all-reduce(f32[4,1152]{1,0:T(4,128)S(1)} %fusion.68), channel_id=1, replica_groups=mesh['seq'=8,'tp'=4] {'tp'}, use_global_device_ids=true, to_apply=%region_32.33 | all-reduce | flops 4608 | bytes 36864 | tf_op jit(solution)/shard_map/psum | solution.py:291
  997.1 2.0 fusion.73
  1001.1 57.7 %reduce-scatter.8.cloned.1.call-done = bf16[4,300,288]{1,2,0:T(8,128)(2,1)} async-done(((bf16[4,300,1152]{1,2,0:T(8,128)(2,1)}), bf16[4,300,288]{1,2,0:T(8,128)(2,1)}) %reduce-scatter.8.cloned.1.call-update) | async-done | bytes 691216 | tf_op jit(solution)/shard_map/reduce_scatter | solution.py:302
  1058.8 2.5 convert_element_type.205
  (261 shorter events, 82.6 us)
Async XLA Ops:
  7.2 6.5 copy-start.1
  7.2 7.5 copy-start.48
  7.2 7.6 copy-start.45
  7.2 22.5 %copy-start.46 = (bf16[144,288]{1,0:T(8,128)(2,1)S(1)}, bf16[144,288]{1,0:T(8,128)(2,1)}, u32[]{:S(2)}) copy-start(bf16[144,288]{1,0:T(8,128)(2,1)} %param.24) | copy-start | bytes 248836
  7.2 52.7 %all-gather.9.cloned.1.call-start = ((), (), s32[]{:S(2)}) async-start(), calls=%async_computation.8 | async-start | bytes 2985984 | tf_op jit(solution)/shard_map/all_gather | solution.py:72
  8.0 78.0 %all-gather.7.cloned.1.call-start = ((), (), s32[]{:S(2)}) async-start(), calls=%async_computation.7 | async-start | bytes 4644864 | tf_op jit(solution)/shard_map/all_gather | solution.py:79
  8.7 34.7 %copy-start.47 = (bf16[288,144]{0,1:T(8,128)(2,1)S(1)}, bf16[288,144]{0,1:T(8,128)(2,1)}, u32[]{:S(2)}) copy-start(bf16[288,144]{0,1:T(8,128)(2,1)} %param.26) | copy-start | bytes 248836
  8.7 114.6 %all-gather.11.cloned.1.call-start = ((), (), s32[]{:S(2)}) async-start(), calls=%async_computation.10 | async-start | bytes 1990656 | tf_op jit(solution)/shard_map/all_gather | solution.py:75
  9.5 188.4 %all-reduce.8.cloned.1.call-start = ((), (), s32[]{:S(2)}) async-start(), calls=%async_computation.9 | async-start | bytes 3538944 | tf_op jit(solution)/shard_map/psum | solution.py:23
  13.6 41.1 %copy-start.17 = (bf16[4,300,1152]{2,0,1:T(4,128)(2,1)S(1)}, bf16[4,300,1152]{2,0,1:T(4,128)(2,1)}, u32[]{:S(2)}) copy-start(bf16[4,300,1152]{2,0,1:T(4,128)(2,1)} %param.17) | copy-start | bytes 8294404
  14.7 71.3 %copy-start.56 = (bf16[4,1152]{1,0:T(4,128)(2,1)}, bf16[4,1152]{1,0:T(4,128)(2,1)S(1)}, u32[]{:S(2)}) copy-start(bf16[4,1152]{1,0:T(4,128)(2,1)S(1)} %multiply_convert_fusion.6) | copy-start | bytes 27652
  29.7 90.2 %copy-start.9 = (bf16[288,1152]{0,1:T(8,128)(2,1)}, bf16[288,1152]{0,1:T(8,128)(2,1)S(1)}, u32[]{:S(2)}) copy-start(bf16[288,1152]{0,1:T(8,128)(2,1)S(1)} %all_gather.30) | copy-start | bytes 1990660
  43.4 156.5 %copy-start.10 = (bf16[1152,288]{1,0:T(8,128)(2,1)}, bf16[1152,288]{1,0:T(8,128)(2,1)S(1)}, u32[]{:S(2)}) copy-start(bf16[1152,288]{1,0:T(8,128)(2,1)S(1)} %all_gather.32) | copy-start | bytes 1990660
  103.3 182.3 %copy-start.31 = (f32[16,1152]{1,0:T(8,128)}, f32[16,1152]{1,0:T(8,128)S(1)}, u32[]{:S(2)}) copy-start(f32[16,1152]{1,0:T(8,128)S(1)} %get-tuple-element.159) | copy-start | bytes 221188
  103.3 185.1 %copy-start.36 = (f32[16,1152]{1,0:T(8,128)}, f32[16,1152]{1,0:T(8,128)S(1)}, u32[]{:S(2)}) copy-start(f32[16,1152]{1,0:T(8,128)S(1)} %get-tuple-element.154) | copy-start | bytes 221188
  104.4 4.6 copy-start.8
  113.3 2.4 copy-start.25
  113.3 5.2 copy-start.27
  113.3 5.2 copy-start.42
  115.7 2.7 copy-start.43
  119.6 2.3 copy-start.18
  120.0 2.2 copy-start.61
  120.0 2.3 copy-start.59
  121.9 163.6 %all-reduce.10.cloned.1.call-start = ((), (), s32[]{:S(2)}) async-start(), calls=%async_computation.11 | async-start | bytes 3538944 | tf_op jit(solution)/shard_map/psum | solution.py:23
  128.9 5.6 copy-start.30
  199.8 3.8 copy-start.13
  203.6 2.4 copy-start
  203.6 2.4 copy-start.54
  203.6 2.5 copy-start.14
  206.1 2.8 copy-start.11
  210.8 105.8 %all-gather.15.cloned.1.call-start = ((), (), s32[]{:S(2)}) async-start(), calls=%async_computation.13 | async-start | bytes 2985984 | tf_op jit(solution)/shard_map/all_gather | solution.py:78
  211.4 137.4 %all-gather.13.cloned.1.call-start = ((), (), s32[]{:S(2)}) async-start(), calls=%async_computation.12 | async-start | bytes 2985984 | tf_op jit(solution)/shard_map/all_gather | solution.py:77
  212.2 223.0 %all-reduce.12.cloned.1.call-start = ((), (), s32[]{:S(2)}) async-start(), calls=%async_computation.14 | async-start | bytes 3538944 | tf_op jit(solution)/shard_map/psum | solution.py:23
  348.8 5.8 copy-start.62
  356.8 3.0 copy-start.55
  356.8 3.0 copy-start.58
  359.5 176.3 %all-reduce.14.cloned.1.call-start = ((), (), s32[]{:S(2)}) async-start(), calls=%async_computation.15 | async-start | bytes 3538944 | tf_op jit(solution)/shard_map/psum | solution.py:23
  435.2 3.3 copy-start.12
  439.1 4.7 copy-start.52
  447.5 4.6 copy-start.20
  447.5 4.6 slice-start
  447.5 4.6 slice-start.1
  461.1 135.5 %all-reduce.16.cloned.1.call-start = ((), (), s32[]{:S(2)}) async-start(), calls=%async_computation.16 | async-start | bytes 2949120 | tf_op jit(solution)/shard_map/psum | solution.py:278
  461.2 2.7 copy-start.21
  469.2 3.1 copy-start.19
  469.2 165.4 %reduce-scatter.16.cloned.1.call-start = ((), (), s32[]{:S(2)}) async-start(), calls=%async_computation.21 | async-start | bytes 995328 | tf_op jit(solution)/shard_map/reduce_scatter | solution.py:315
  472.2 63.6 %copy-start.53 = (f32[16,17]{1,0:T(8,128)S(1)}, f32[16,17]{1,0:T(8,128)}, u32[]{:S(2)}) copy-start(f32[16,17]{1,0:T(8,128)} %copy-done.52) | copy-start | bytes 3268
  472.2 200.7 %reduce-scatter.14.cloned.1.call-start = ((), (), s32[]{:S(2)}) async-start(), calls=%async_computation.20 | async-start | bytes 995328 | tf_op jit(solution)/shard_map/reduce_scatter | solution.py:312
  475.9 65.0 %copy-start.32 = (f32[16,1152]{1,0:T(8,128)S(1)}, f32[16,1152]{1,0:T(8,128)}, u32[]{:S(2)}) copy-start(f32[16,1152]{1,0:T(8,128)} %copy-done.31) | copy-start | bytes 221188
  476.0 236.2 %reduce-scatter.12.cloned.1.call-start = ((), (), s32[]{:S(2)}) async-start(), calls=%async_computation.19 | async-start | bytes 995328 | tf_op jit(solution)/shard_map/reduce_scatter | solution.py:309
  540.9 3.3 copy-start.34
  547.0 212.3 %reduce-scatter.18.cloned.1.call-start = ((), (), s32[]{:S(2)}) async-start(), calls=%async_computation.22 | async-start | bytes 2985984 | tf_op jit(solution)/shard_map/reduce_scatter | solution.py:318
  551.9 254.9 %reduce-scatter.20.cloned.1.call-start = ((), (), s32[]{:S(2)}) async-start(), calls=%async_computation.23 | async-start | bytes 2985984 | tf_op jit(solution)/shard_map/reduce_scatter | solution.py:321
  556.7 387.1 %all-reduce.18.cloned.1.call-start = ((), (), s32[]{:S(2)}) async-start(), calls=%async_computation.24 | async-start | bytes 7077888 | tf_op jit(solution)/shard_map/psum | solution.py:23
  564.0 2.8 copy-start.44
  568.8 1.8 copy-start.16
  581.9 417.3 %reduce-scatter.10.cloned.1.call-start = ((), (), s32[]{:S(2)}) async-start(), calls=%async_computation.18 | async-start | bytes 2985984 | tf_op jit(solution)/shard_map/reduce_scatter | solution.py:306
  591.9 466.9 %reduce-scatter.8.cloned.1.call-start = ((), (), s32[]{:S(2)}) async-start(), calls=%async_computation.17 | async-start | bytes 4423680 | tf_op jit(solution)/shard_map/reduce_scatter | solution.py:302
  611.1 332.8 %copy-start.23 = (f32[16,1152]{1,0:T(8,128)S(1)}, f32[16,1152]{1,0:T(8,128)}, u32[]{:S(2)}) copy-start(f32[16,1152]{1,0:T(8,128)} %copy-done.22) | copy-start | bytes 221188
  761.2 184.8 %copy-start.51 = (f32[16,17]{1,0:T(8,128)S(1)}, f32[16,17]{1,0:T(8,128)}, u32[]{:S(2)}) copy-start(f32[16,17]{1,0:T(8,128)} %copy-done.50) | copy-start | bytes 3268
  943.9 2.1 copy-start.5
  947.5 1.6 copy-start.24
  947.5 1.6 copy-start.37
  949.9 26.2 %copy-start.49 = (f32[4,1152]{1,0:T(4,128)S(1)}, f32[4,1152]{1,0:T(4,128)}, u32[]{:S(2)}) copy-start(f32[4,1152]{1,0:T(4,128)} %param.18) | copy-start | bytes 55300
  (20 other events, 21.3 us)
Sparse Core Ops, SparseCore 0:
  10.0 37.6 all-gather.8
  49.5 36.4 all-gather.6
  87.9 26.5 all-gather.10
  122.0 75.7 all-reduce.7
  211.0 74.5 all-reduce.9
  287.3 29.2 all-gather.14
  318.5 30.2 all-gather.12
  359.6 75.5 all-reduce.11
  461.2 74.5 all-reduce.13
  538.9 57.6 all-reduce.15
  600.2 34.3 reduce-scatter.15
  637.7 35.1 reduce-scatter.13
  677.0 35.0 reduce-scatter.11
  715.5 43.7 reduce-scatter.17
  763.0 43.7 reduce-scatter.19
  809.7 134.1 all-reduce.17
  947.2 42.9 reduce-scatter.9
  992.4 66.3 reduce-scatter.7
where the time goes:
time: 1080 us; the launch traced here: 1070 us
  waiting for transfers between devices  733 us (68%)
  matrix products  105 us (10%)
  blocking collectives  95.8 us (9%)
  local copies, waits for them, and re-layouts  71.9 us (7%)
  other arithmetic  45.7 us (4%)
  between operations  15.4 us (1%)
    psum x5, waiting for transfers between devices, total_rows(): return lax.psum(partial_value, 'tp')  407 us
    reduce_scatter x1, waiting for transfers between devices, shards(): lax.psum_scatter(caption_part.astype(jnp.bfloat16), 'tp', scatter_dimensi...  57.7 us
    reduce_scatter x1, waiting for transfers between devices, shards(): lax.psum_scatter(grad_down.astype(jnp.bfloat16), 'seq', scatter_dimension...  45.7 us
    reduce_scatter x1, waiting for transfers between devices, shards(): lax.psum_scatter(grad_up.astype(jnp.bfloat16), 'seq', scatter_dimension=0...  45.6 us
    reduce_scatter x1, waiting for transfers between devices, shards(): lax.psum_scatter(grad_out.astype(jnp.bfloat16), 'seq', scatter_dimension=...  37.7 us
    reduce_scatter x1, waiting for transfers between devices, shards(): lax.psum_scatter(grad_query2.astype(jnp.bfloat16), 'seq', scatter_dimensi...  36.7 us
    all_gather x1, waiting for transfers between devices, shards(): lax.all_gather(w_up, 'seq', axis=0, tiled=True)  28.1 us
    psum x1, blocking collectives, shards(): lax.psum(d_mods.astype(jnp.bfloat16), 'seq').astype(jnp.float32)  24.9 us
  transfers between devices with their start and end apart: 18, of which 15 were waited for; matrix products, arithmetic and copies ran while one was open for 15% of the time, Pallas kernels for 0%

commit v1 on v0

--- a/solution.py
+++ b/solution.py
@@ -8,6 +8,19 @@
 EPSILON = 1e-06
 NEG_FILL = -1e30
 HIGHEST = lax.Precision.HIGHEST
+
+
+def ring_gather(x, axis, dim):
+    ways = lax.axis_size(axis)
+    up = [(d, (d + 1) % ways) for d in range(ways)]
+    down = [(d, (d - 1) % ways) for d in range(ways)]
+    earlier, later = ([x], [x])
+    for _ in range(ways // 2):
+        earlier.append(lax.ppermute(earlier[-1], axis, up))
+    for _ in range((ways - 1) // 2):
+        later.append(lax.ppermute(later[-1], axis, down))
+    line = jnp.concatenate([*earlier[::-1], *later[1:]], axis=dim)
+    return jnp.roll(line, (lax.axis_index(axis) - ways // 2) * x.shape[dim], axis=dim)
 
 
 def normalize(rows):
@@ -74,7 +87,7 @@
         lax.all_gather(w_query2, "seq", axis=0, tiled=True),
         lax.all_gather(w_kv2, "seq", axis=0, tiled=True),
         lax.all_gather(w_out2, "seq", axis=1, tiled=True),
-        lax.all_gather(w_up, "seq", axis=0, tiled=True),
+        ring_gather(w_up, "seq", 0),
         lax.all_gather(w_down, "seq", axis=1, tiled=True),
         lax.all_gather(w_ada, "seq", axis=0, tiled=True),
     )

time: 1080 us -> 1040 us (0.963)
  waiting for transfers between devices: 733 us -> 671 us
  local copies, waits for them, and re-layouts: 71.9 us -> 86.7 us
    psum x5, waiting for transfers between devices: 407 us -> 344 us  [total_rows(): return lax.psum(partial_value, 'tp')]
    all_gather x1 -> x0, waiting for transfers between devices: 28.1 us -> none  [shards(): lax.all_gather(w_up, 'seq', axis=0, tiled=True)]
    ppermute x0 -> x7, waiting for transfers between devices: none -> 21.5 us  [the longest x4 21.5 us: ring_gather(): earlier.append(lax.ppermute(earlier[-1], axis, up))]
    all_gather x1, waiting for transfers between devices: 21.2 us -> 0.59 us  [shards(): lax.all_gather(w_down, 'seq', axis=1, tiled=True)]
    unnamed x142 -> x149, local copies, waits for them, and re-layouts: 15.6 us -> 34.4 us
    all_gather x1, waiting for transfers between devices: 0.01 us -> 16.8 us  [shards(): lax.all_gather(w_qkv, 'seq', axis=0, tiled=True)]
    all_gather x1, waiting for transfers between devices: 21.8 us -> 34.1 us  [shards(): lax.all_gather(w_ada, 'seq', axis=0, tiled=True)]
  transfers between devices with their start and end apart: 18 -> 24, of which waited for: 15 -> 17; matrix products, arithmetic and copies ran while one was open for 15% -> 18% of each run, Pallas kernels for 0% -> 0%
where the time goes in v1:
time: 1040 us; the launch traced here: 1030 us
  waiting for transfers between devices  671 us (65%)
  matrix products  105 us (10%)
  blocking collectives  92.8 us (9%)
  local copies, waits for them, and re-layouts  86.7 us (8%)
  other arithmetic  46.6 us (4%)
  between operations  15.1 us (1%)
    psum x5, waiting for transfers between devices, total_rows(): return lax.psum(partial_value, 'tp')  344 us
    reduce_scatter x1, waiting for transfers between devices, shards(): lax.psum_scatter(caption_part.astype(jnp.bfloat16), 'tp', scatter_dimensi...  57.7 us
    reduce_scatter x1, waiting for transfers between devices, shards(): lax.psum_scatter(grad_up.astype(jnp.bfloat16), 'seq', scatter_dimension=0...  45.7 us
    reduce_scatter x1, waiting for transfers between devices, shards(): lax.psum_scatter(grad_down.astype(jnp.bfloat16), 'seq', scatter_dimension...  45.7 us
    reduce_scatter x1, waiting for transfers between devices, shards(): lax.psum_scatter(grad_out.astype(jnp.bfloat16), 'seq', scatter_dimension=...  37.5 us
    reduce_scatter x1, waiting for transfers between devices, shards(): lax.psum_scatter(grad_query2.astype(jnp.bfloat16), 'seq', scatter_dimensi...  36.8 us
    unnamed x149, local copies, waits for them, and re-layouts  34.4 us
    all_gather x1, waiting for transfers between devices, shards(): lax.all_gather(w_ada, 'seq', axis=0, tiled=True)  34.1 us
  transfers between devices with their start and end apart: 24, of which 17 were waited for; matrix products, arithmetic and copies ran while one was open for 18% of the time, Pallas kernels for 0%

profile of v1, /device:TPU:0, one launch (start us, length us, event | category | flops | bytes accessed | tf_op | source)
XLA Modules:
  0.0 1026.7 jit_solution(6933198774202900546)
XLA Ops:
  13.4 14.2 %all_gather.27 = bf16[288,1152]{0,1:T(8,128)(2,1)S(1)} all-gather(bf16[288,144]{0,1:T(8,128)(2,1)S(1)} %copy-done.48), channel_id=1, replica_groups=mesh['seq'=8,'tp'=4] {'seq'}, dimensions={1}, use_global_device_ids=true | all-gather | bytes 746496 | tf_op jit(solution)/shard_map/all_gather | solution.py:86
  27.6 16.8 %all-gather.8.cloned.1.call-done = bf16[1152,3,288]{2,0,1:T(8,128)(2,1)} async-done(((bf16[144,3,288]{2,0,1:T(8,128)(2,1)}), bf16[1152,3,288]{2,0,1:T(8,128)(2,1)}) %all-gather.8.cloned.1.call-update) | async-done | bytes 1990672 | tf_op jit(solution)/shard_map/all_gather | solution.py:85
  44.4 4.2 copy.144
  48.7 34.1 %all-gather.6.cloned.1.call-done = bf16[1152,1728]{1,0:T(8,128)(2,1)} async-done(((bf16[144,1728]{1,0:T(8,128)(2,1)}), bf16[1152,1728]{1,0:T(8,128)(2,1)}) %all-gather.6.cloned.1.call-update) | async-done | bytes 3981328 | tf_op jit(solution)/shard_map/all_gather | solution.py:92
  82.8 2.8 convolution_bitcast_fusion
  85.6 13.4 %all-gather = f32[4,1728,4]{1,2,0:T(4,128)S(1)} all-gather(f32[1,1728,4]{1,2,0:T(4,128)S(1)} %convolution_bitcast_fusion), channel_id=1, replica_groups=mesh['seq'=8,'tp'=4] {'tp'}, dimensions={0}, use_global_device_ids=true | all-gather | bytes 138240 | tf_op jit(solution)/shard_map/all_gather | solution.py:98
  101.4 3.4 convolution_convert_fusion.9
  104.8 2.3 reshape.347
  113.4 2.6 collective-permute-start.4
  116.1 7.8 collective-permute-done
  128.1 12.1 %all_gather.29 = bf16[1152,288]{1,0:T(8,128)(2,1)S(1)} all-gather(bf16[144,288]{1,0:T(8,128)(2,1)} %param.24), channel_id=1, replica_groups=mesh['seq'=8,'tp'=4] {'seq'}, dimensions={0}, use_global_device_ids=true | all-gather | bytes 746496 | tf_op jit(solution)/shard_map/all_gather | solution.py:87
  140.1 10.6 %all_gather.30 = bf16[288,1152]{0,1:T(8,128)(2,1)S(1)} all-gather(bf16[288,144]{0,1:T(8,128)(2,1)} %param.26), channel_id=1, replica_groups=mesh['seq'=8,'tp'=4] {'seq'}, dimensions={1}, use_global_device_ids=true | all-gather | bytes 746496 | tf_op jit(solution)/shard_map/all_gather | solution.py:89
  151.3 2.3 collective-permute-start.5
  153.6 7.3 collective-permute-done.2
  161.9 2.8 collective-permute-start.6
  164.7 6.4 collective-permute-done.3
  189.6 6.6 copy.152
  196.2 5.6 convolution_convert_fusion.4
  201.8 2.6 fusion.45
  208.2 2.6 fusion.104
  220.8 3.9 fusion.105
  224.8 74.6 %all-reduce.10.cloned.1.call-done = f32[16,17,1152]{2,1,0:T(8,128)} async-done(((f32[16,17,1152]{2,1,0:T(8,128)}), f32[16,17,1152]{2,1,0:T(8,128)}) %all-reduce.10.cloned.1.call-update) | async-done | bytes 1253392 | tf_op jit(solution)/shard_map/psum | solution.py:36
  299.4 2.5 fusion.100
  304.1 2.2 reshape.352
  306.3 5.2 fusion.40
  312.4 4.0 fusion.19
  316.4 2.7 reshape.355
  319.4 74.4 %all-reduce.12.cloned.1.call-done = f32[16,17,1152]{2,1,0:T(8,128)} async-done(((f32[16,17,1152]{2,1,0:T(8,128)}), f32[16,17,1152]{2,1,0:T(8,128)}) %all-reduce.12.cloned.1.call-update) | async-done | bytes 1253392 | tf_op jit(solution)/shard_map/psum | solution.py:36
  393.8 3.2 multiply_reduce_fusion.2
  400.3 2.2 reshape.356
  402.5 2.6 convolution_convert_fusion.12
  406.2 4.6 multiply_reduce_fusion
  416.6 3.1 fusion.48
  419.9 2.7 fusion.15
  422.5 4.0 fusion.16
  427.9 2.9 convolution_convert_fusion.5
  431.8 2.8 convolution_convert_fusion.6
  434.7 59.8 %all-reduce.14.cloned.1.call-done = f32[16,17,1152]{2,1,0:T(8,128)} async-done(((f32[16,17,1152]{2,1,0:T(8,128)}), f32[16,17,1152]{2,1,0:T(8,128)}) %all-reduce.14.cloned.1.call-update) | async-done | bytes 1253392 | tf_op jit(solution)/shard_map/psum | solution.py:36
  494.5 3.9 multiply_reduce_fusion.3
  500.7 2.2 reshape.357
  502.9 2.7 convolution_convert_fusion.7
  506.1 4.5 convolution_convert_fusion.1
  510.7 4.8 convolution_convert_fusion
  515.6 4.5 fusion.97
  520.1 2.7 reshape.353
  533.4 2.9 reshape.378
  536.3 4.3 fusion.106
  540.8 2.2 reshape.375
  546.0 4.4 convolution_convert_fusion.3
  550.5 4.9 all-reduce.16.cloned.1.call-done
  555.5 2.6 fusion.56
  559.1 4.2 dot_general.164
  563.3 6.6 convolution_convert_fusion.2
  569.9 23.4 %reduce-scatter.16.cloned.1.call-done = bf16[288,144]{0,1:T(8,128)(2,1)} async-done(((bf16[288,1152]{0,1:T(8,128)(2,1)}), bf16[288,144]{0,1:T(8,128)(2,1)}) %reduce-scatter.16.cloned.1.call-update) | async-done | bytes 82960 | tf_op jit(solution)/shard_map/reduce_scatter | solution.py:328
  594.9 36.8 %reduce-scatter.14.cloned.1.call-done = bf16[144,288]{1,0:T(8,128)(2,1)} async-done(((bf16[1152,288]{1,0:T(8,128)(2,1)}), bf16[144,288]{1,0:T(8,128)(2,1)}) %reduce-scatter.14.cloned.1.call-update) | async-done | bytes 82960 | tf_op jit(solution)/shard_map/reduce_scatter | solution.py:325
  633.3 37.5 %reduce-scatter.12.cloned.1.call-done = bf16[288,144]{0,1:T(8,128)(2,1)} async-done(((bf16[288,1152]{0,1:T(8,128)(2,1)}), bf16[288,144]{0,1:T(8,128)(2,1)}) %reduce-scatter.12.cloned.1.call-update) | async-done | bytes 82960 | tf_op jit(solution)/shard_map/reduce_scatter | solution.py:322
  672.3 45.7 %reduce-scatter.18.cloned.1.call-done = bf16[144,1152]{1,0:T(8,128)(2,1)} async-done(((bf16[1152,1152]{1,0:T(8,128)(2,1)}), bf16[144,1152]{1,0:T(8,128)(2,1)}) %reduce-scatter.18.cloned.1.call-update) | async-done | bytes 331792 | tf_op jit(solution)/shard_map/reduce_scatter | solution.py:331
  719.9 45.7 %reduce-scatter.20.cloned.1.call-done = bf16[1152,144]{0,1:T(8,128)(2,1)} async-done(((bf16[1152,1152]{0,1:T(8,128)(2,1)}), bf16[1152,144]{0,1:T(8,128)(2,1)}) %reduce-scatter.20.cloned.1.call-update) | async-done | bytes 331792 | tf_op jit(solution)/shard_map/reduce_scatter | solution.py:334
  767.4 135.2 %all-reduce.18.cloned.1.call-done = (f32[16,17,1152]{2,1,0:T(8,128)}, f32[16,17,1152]{2,1,0:T(8,128)}) async-done(((f32[16,17,1152]{2,1,0:T(8,128)}, f32[16,17,1152]{2,1,0:T(8,128)}), (f32[16,17,1152]{2,1,0:T(8,128)}, f32[16,17,1152]{2,1,0:T(8,128)})) %all-reduce.18.cloned.1.call-update) | async-done | bytes 2506768 | tf_op jit(solution)/shard_map/psum | solution.py:36
  910.0 24.9 %psum.70 = bf16[4,6912]{1,0:T(4,128)(2,1)S(1)} all-reduce(bf16[4,6912]{1,0:T(4,128)(2,1)S(1)} %bitcast.194), channel_id=1, replica_groups=mesh['seq'=8,'tp'=4] {'seq'}, use_global_device_ids=true, to_apply=%region_31.32 | all-reduce | flops 27648 | bytes 110592 | tf_op jit(solution)/shard_map/psum | solution.py:292
  934.9 3.4 fusion.72
  938.2 17.6 %psum.71 = f32[4,1152]{1,0:T(4,128)} all-reduce(f32[4,1152]{1,0:T(4,128)S(1)} %fusion.72), channel_id=1, replica_groups=mesh['seq'=8,'tp'=4] {'tp'}, use_global_device_ids=true, to_apply=%region_32.33 | all-reduce | flops 4608 | bytes 36864 | tf_op jit(solution)/shard_map/psum | solution.py:304
  959.8 57.7 %reduce-scatter.8.cloned.1.call-done = bf16[4,300,288]{1,2,0:T(8,128)(2,1)} async-done(((bf16[4,300,1152]{1,2,0:T(8,128)(2,1)}), bf16[4,300,288]{1,2,0:T(8,128)(2,1)}) %reduce-scatter.8.cloned.1.call-update) | async-done | bytes 691216 | tf_op jit(solution)/shard_map/reduce_scatter | solution.py:315
  1017.5 2.5 convert_element_type.205
  (280 shorter events, 105.9 us)
Async XLA Ops:
  7.2 6.0 copy-start.55
  7.2 5.0 copy-start.1
  7.2 6.0 copy-start.58
  7.2 6.2 copy-start.48
  7.2 37.2 %all-gather.8.cloned.1.call-start = ((), (), s32[]{:S(2)}) async-start(), calls=%async_computation.8 | async-start | bytes 2985984 | tf_op jit(solution)/shard_map/all_gather | solution.py:85
  8.0 74.8 %all-gather.6.cloned.1.call-start = ((), (), s32[]{:S(2)}) async-start(), calls=%async_computation.7 | async-start | bytes 4644864 | tf_op jit(solution)/shard_map/all_gather | solution.py:92
  8.7 180.9 %all-gather.10.cloned.1.call-start = ((), (), s32[]{:S(2)}) async-start(), calls=%async_computation.10 | async-start | bytes 1990656 | tf_op jit(solution)/shard_map/all_gather | solution.py:88
  9.4 192.3 %all-reduce.8.cloned.1.call-start = ((), (), s32[]{:S(2)}) async-start(), calls=%async_computation.9 | async-start | bytes 3538944 | tf_op jit(solution)/shard_map/psum | solution.py:36
  10.2 72.6 %copy-start.54 = (bf16[4,1152]{1,0:T(4,128)(2,1)}, bf16[4,1152]{1,0:T(4,128)(2,1)S(1)}, u32[]{:S(2)}) copy-start(bf16[4,1152]{1,0:T(4,128)(2,1)S(1)} %multiply_convert_fusion.6) | copy-start | bytes 27652
  27.6 83.8 %copy-start.9 = (bf16[288,1152]{0,1:T(8,128)(2,1)}, bf16[288,1152]{0,1:T(8,128)(2,1)S(1)}, u32[]{:S(2)}) copy-start(bf16[288,1152]{0,1:T(8,128)(2,1)S(1)} %all_gather.27) | copy-start | bytes 1990660
  100.1 199.3 %copy-start.32 = (f32[16,1152]{1,0:T(8,128)}, f32[16,1152]{1,0:T(8,128)S(1)}, u32[]{:S(2)}) copy-start(f32[16,1152]{1,0:T(8,128)S(1)} %get-tuple-element.159) | copy-start | bytes 221188
  101.2 3.6 copy-start.8
  108.1 2.2 copy-start.45
  111.0 2.3 copy-start.17
  113.3 107.6 %all-gather.12.cloned.1.call-start = ((), (), s32[]{:S(2)}) async-start(), calls=%async_computation.12 | async-start | bytes 2985984 | tf_op jit(solution)/shard_map/all_gather | solution.py:91
  113.3 10.6 %collective-permute-start = (bf16[144,1152]{1,0:T(8,128)(2,1)}, bf16[144,1152]{1,0:T(8,128)(2,1)}, u32[]{:S(2)}, u32[]{:S(2)}) collective-permute-start(bf16[144,1152]{1,0:T(8,128)(2,1)} %param.27), channel_id=1, source_target_pairs={{0,4},{4,8},{8,12},{12,16},{16,20},{20,24},{24,28},{28,0},{1,5},{5... | collective-permute-start | bytes 995336 | tf_op jit(solution)/shard_map/ppermute | solution.py:19
  113.4 37.9 %collective-permute-start.4 = (bf16[144,1152]{1,0:T(8,128)(2,1)}, bf16[144,1152]{1,0:T(8,128)(2,1)}, u32[]{:S(2)}, u32[]{:S(2)}) collective-permute-start(bf16[144,1152]{1,0:T(8,128)(2,1)} %param.27), channel_id=1, source_target_pairs={{0,28},{4,0},{8,4},{12,8},{16,12},{20,16},{24,20},{28,24},{1,29},{... | collective-permute-start | bytes 995336 | tf_op jit(solution)/shard_map/ppermute | solution.py:21
  116.0 183.3 %all-reduce.10.cloned.1.call-start = ((), (), s32[]{:S(2)}) async-start(), calls=%async_computation.11 | async-start | bytes 3538944 | tf_op jit(solution)/shard_map/psum | solution.py:36
  123.9 26.8 %collective-permute-start.1 = (bf16[144,1152]{1,0:T(8,128)(2,1)}, bf16[144,1152]{1,0:T(8,128)(2,1)}, u32[]{:S(2)}, u32[]{:S(2)}) collective-permute-start(bf16[144,1152]{1,0:T(8,128)(2,1)} %collective-permute-done), channel_id=1, source_target_pairs={{0,4},{4,8},{8,12},{12,16},{16,20},{20,24},{24,28},{28,0},{1,5},{5... | collective-permute-start | bytes 995336 | tf_op jit(solution)/shard_map/ppermute | solution.py:19
  127.9 23.3 %copy-start.57 = (s32[4]{0:T(128)S(1)}, s32[4]{0:T(128)}, u32[]{:S(2)}) copy-start(s32[4]{0:T(128)} %param.20) | copy-start | bytes 52
  140.1 65.7 %copy-start.10 = (bf16[1152,288]{1,0:T(8,128)(2,1)}, bf16[1152,288]{1,0:T(8,128)(2,1)S(1)}, u32[]{:S(2)}) copy-start(bf16[1152,288]{1,0:T(8,128)(2,1)S(1)} %all_gather.29) | copy-start | bytes 1990660
  150.7 65.3 %copy-start.11 = (bf16[288,1152]{0,1:T(8,128)(2,1)}, bf16[288,1152]{0,1:T(8,128)(2,1)S(1)}, u32[]{:S(2)}) copy-start(bf16[288,1152]{0,1:T(8,128)(2,1)S(1)} %all_gather.30) | copy-start | bytes 1990660
  150.8 10.1 collective-permute-start.2
  151.3 10.6 %collective-permute-start.5 = (bf16[144,1152]{1,0:T(8,128)(2,1)}, bf16[144,1152]{1,0:T(8,128)(2,1)S(1)}, u32[]{:S(2)}, u32[]{:S(2)}) collective-permute-start(bf16[144,1152]{1,0:T(8,128)(2,1)} %collective-permute-done.4), channel_id=1, source_target_pairs={{0,28},{4,0},{8,4},{12,8},{16,12},{20,16},{24,20},{28,24},{1,29},{... | collective-permute-start | bytes 995336 | tf_op jit(solution)/shard_map/ppermute | solution.py:21
  160.8 10.2 collective-permute-start.3
  161.9 17.7 %copy-start.28 = (bf16[144,1152]{1,0:T(8,128)(2,1)}, bf16[144,1152]{1,0:T(8,128)(2,1)S(1)}, u32[]{:S(2)}) copy-start(bf16[144,1152]{1,0:T(8,128)(2,1)S(1)} %collective-permute-done.5) | copy-start | bytes 995332
  161.9 18.4 %collective-permute-start.6 = (bf16[144,1152]{1,0:T(8,128)(2,1)S(1)}, bf16[144,1152]{1,0:T(8,128)(2,1)S(1)}, u32[]{:S(2)}, u32[]{:S(2)}) collective-permute-start(bf16[144,1152]{1,0:T(8,128)(2,1)S(1)} %collective-permute-done.5), channel_id=1, source_target_pairs={{0,28},{4,0},{8,4},{12,8},{16,12},{20,16},{24,20},{28,24},{1,29},{... | collective-permute-start | bytes 995336 | tf_op jit(solution)/shard_map/ppermute | solution.py:21
  180.3 7.6 copy-start.30
  205.8 4.9 copy-start.13
  210.8 2.4 copy-start
  210.8 2.5 copy-start.14
  216.1 2.0 copy-start.29
  218.0 1.7 copy-start.7
  218.0 1.7 copy-start.38
  218.0 175.8 %all-reduce.12.cloned.1.call-start = ((), (), s32[]{:S(2)}) async-start(), calls=%async_computation.13 | async-start | bytes 3538944 | tf_op jit(solution)/shard_map/psum | solution.py:36
  220.2 4.6 copy-start.40
  319.1 175.4 %all-reduce.14.cloned.1.call-start = ((), (), s32[]{:S(2)}) async-start(), calls=%async_computation.14 | async-start | bytes 3538944 | tf_op jit(solution)/shard_map/psum | solution.py:36
  393.8 3.2 copy-start.12
  397.7 4.8 copy-start.52
  406.2 4.6 copy-start.19
  406.2 4.6 slice-start
  406.2 4.6 slice-start.1
  419.8 135.6 %all-reduce.16.cloned.1.call-start = ((), (), s32[]{:S(2)}) async-start(), calls=%async_computation.15 | async-start | bytes 2949120 | tf_op jit(solution)/shard_map/psum | solution.py:291
  419.9 2.7 copy-start.20
  427.8 3.1 copy-start.18
  427.9 165.4 %reduce-scatter.16.cloned.1.call-start = ((), (), s32[]{:S(2)}) async-start(), calls=%async_computation.20 | async-start | bytes 995328 | tf_op jit(solution)/shard_map/reduce_scatter | solution.py:328
  430.9 63.6 %copy-start.53 = (f32[16,17]{1,0:T(8,128)S(1)}, f32[16,17]{1,0:T(8,128)}, u32[]{:S(2)}) copy-start(f32[16,17]{1,0:T(8,128)} %copy-done.52) | copy-start | bytes 3268
  430.9 200.8 %reduce-scatter.14.cloned.1.call-start = ((), (), s32[]{:S(2)}) async-start(), calls=%async_computation.19 | async-start | bytes 995328 | tf_op jit(solution)/shard_map/reduce_scatter | solution.py:325
  434.6 65.0 %copy-start.33 = (f32[16,1152]{1,0:T(8,128)S(1)}, f32[16,1152]{1,0:T(8,128)}, u32[]{:S(2)}) copy-start(f32[16,1152]{1,0:T(8,128)} %copy-done.32) | copy-start | bytes 221188
  434.6 236.1 %reduce-scatter.12.cloned.1.call-start = ((), (), s32[]{:S(2)}) async-start(), calls=%async_computation.18 | async-start | bytes 995328 | tf_op jit(solution)/shard_map/reduce_scatter | solution.py:322
  499.6 3.3 copy-start.36
  505.7 212.4 %reduce-scatter.18.cloned.1.call-start = ((), (), s32[]{:S(2)}) async-start(), calls=%async_computation.21 | async-start | bytes 2985984 | tf_op jit(solution)/shard_map/reduce_scatter | solution.py:331
  510.6 254.9 %reduce-scatter.20.cloned.1.call-start = ((), (), s32[]{:S(2)}) async-start(), calls=%async_computation.22 | async-start | bytes 2985984 | tf_op jit(solution)/shard_map/reduce_scatter | solution.py:334
  515.5 387.1 %all-reduce.18.cloned.1.call-start = ((), (), s32[]{:S(2)}) async-start(), calls=%async_computation.23 | async-start | bytes 7077888 | tf_op jit(solution)/shard_map/psum | solution.py:36
  522.7 2.8 copy-start.47
  527.4 1.8 copy-start.16
  540.5 417.4 %reduce-scatter.10.cloned.1.call-start = ((), (), s32[]{:S(2)}) async-start(), calls=%async_computation.17 | async-start | bytes 2985984 | tf_op jit(solution)/shard_map/reduce_scatter | solution.py:319
  550.5 467.0 %reduce-scatter.8.cloned.1.call-start = ((), (), s32[]{:S(2)}) async-start(), calls=%async_computation.16 | async-start | bytes 4423680 | tf_op jit(solution)/shard_map/reduce_scatter | solution.py:315
  569.9 332.7 %copy-start.22 = (f32[16,1152]{1,0:T(8,128)S(1)}, f32[16,1152]{1,0:T(8,128)}, u32[]{:S(2)}) copy-start(f32[16,1152]{1,0:T(8,128)} %copy-done.21) | copy-start | bytes 221188
  719.9 184.8 %copy-start.51 = (f32[16,17]{1,0:T(8,128)S(1)}, f32[16,17]{1,0:T(8,128)}, u32[]{:S(2)}) copy-start(f32[16,17]{1,0:T(8,128)} %copy-done.50) | copy-start | bytes 3268
  902.6 2.1 copy-start.5
  906.2 1.6 copy-start.23
  906.2 1.6 copy-start.39
  908.7 26.2 %copy-start.49 = (f32[4,1152]{1,0:T(4,128)S(1)}, f32[4,1152]{1,0:T(4,128)}, u32[]{:S(2)}) copy-start(f32[4,1152]{1,0:T(4,128)} %param.18) | copy-start | bytes 55300
  (22 other events, 21.8 us)
Sparse Core Ops, SparseCore 0:
  10.0 34.4 all-gather.7
  46.3 36.4 all-gather.5
  84.7 26.5 all-gather.9
  114.1 75.5 all-reduce.7
  191.5 29.2 all-gather.11
  223.8 75.5 all-reduce.9
  319.3 74.5 all-reduce.11
  419.9 74.5 all-reduce.13
  497.8 57.6 all-reduce.15
  558.9 34.3 reduce-scatter.15
  596.5 35.0 reduce-scatter.13
  635.7 35.0 reduce-scatter.11
  674.2 43.7 reduce-scatter.17
  721.8 43.7 reduce-scatter.19
  768.4 134.1 all-reduce.17
  905.9 42.9 reduce-scatter.9
  951.2 66.3 reduce-scatter.7
